TPU v7x, 512 devices: a whole 4x8x8 slice. The times are simulated.
512 devices in a mesh: lon: 32 (over x, y), lat: 4 (over z_lo, core), lev: 4 (over z_hi).
Axes of the slice: x: 4, y: 8, z: 8 (z_hi: 4, z_lo: 2; z = z_hi * 2 + z_lo), core: 2. Of those that a mesh axis runs over, the one named last changes fastest.
Arguments:
- adjoint_field: float32 [12, 12, 128, 4096], P(None, 'lev', 'lat', 'lon'), may hold values from -6 to 6
- east_courant: float32 [12, 128, 4096], P('lev', 'lat', 'lon'), may hold values from -0.2 to 0.2
- north_courant: float32 [12, 128, 4096], P('lev', 'lat', 'lon'), may hold values from -0.2 to 0.2
- pole_courant: float32 [12, 4096], P('lev', 'lon'), may hold values from -0.2 to 0.2
- mix_fraction: float32 [12, 128, 4096], P('lev', 'lat', 'lon'), may hold values from 0.05 to 0.6
- detrain_share: float32 [12, 128, 4096], P('lev', 'lat', 'lon'), may hold values from 0.1 to 3
- sounding_owner: int32 [2, 32768, 1], P(None, ('lon', 'lat')), may hold values from 0 to 127; in each aligned block of 256 rows (0 to 255, 256 to 511, ..., all dimensions but the last counted through in order) at most 4 rows name the same one
- sounding_cell: int32 [2, 32768], P(None, ('lon', 'lat')), may hold values from 0 to 4095
- sounding_count: int32 [2, 128], P(None, ('lon', 'lat')), may hold values from 1 to 256, 20480 in all within a row
- sounding_forcing: float32 [2, 12, 32768], P(None, 'lev', ('lon', 'lat')), may hold values from -6 to 6
Outputs:
- earlier_adjoint: float32 [12, 12, 128, 4096], P(None, 'lev', 'lat', 'lon')
Inputs may be any that keep to these rules, and one draw needn't show every extreme that they name: `sounding_owner`: in each aligned block of 256 slots of one step (the slots of one device) no owner is named more than 4 times, a bound that some block reaches. `sounding_count`: each step's counts sum to 20480; at each step some device has exactly 256.
All inputs are finite; a program needn't handle non-finite values.
Results may differ from a plain program's by a relative error of at most 0.0001.
Values sent between devices are 32-bit elements; how exact they have to be, the bound alone decides.
A program may use at most 128 MiB of HBM per device.

v0:
```python
import jax
import jax.numpy as jnp
from jax import lax
from jax.sharding import PartitionSpec as P


def from_behind(value, axis, steps):
    count = lax.axis_size(axis)
    pairs = [(source, (source + steps) % count) for source in range(count)]
    return lax.ppermute(value, axis, pairs)


def from_behind_2(block, axis, distance):
    devices = range(lax.axis_size(axis))
    route = [(i - distance, i) for i in devices if i - distance in devices]
    return lax.ppermute(block, axis, route)


def extended(x, sides, width, wrap):
    for axis, dim in sides:
        size, length = (lax.axis_size(axis), x.shape[dim])
        up = [(i, (i + 1) % size) for i in range(size if wrap else size - 1)]
        down = [(j, i) for i, j in up]
        last = lax.slice_in_dim(x, length - width, length, axis=dim)
        initial = lax.slice_in_dim(x, 0, width, axis=dim)
        before = lax.ppermute(last, axis, up)
        after = lax.ppermute(initial, axis, down)
        x = jnp.concatenate([before, x, after], axis=dim)
    return x


def mix_sum(partial_sum):
    return lax.psum(partial_sum, "lev")


def on_device(
    adjoint_field,
    east_courant,
    north_courant,
    pole_courant,
    mix_fraction,
    detrain_share,
    sounding_owner,
    sounding_cell,
    sounding_count,
    sounding_forcing,
):
    lon_count = lax.axis_size("lon")
    lat_count = lax.axis_size("lat")
    lat_place = lax.axis_index("lat")
    owner_self = lax.axis_index("lon") * lat_count + lat_place
    tracers, lev_dev, lat_rows, lon_cols = adjoint_field.shape
    step_count = sounding_forcing.shape[0]
    slot_count = sounding_forcing.shape[2]
    grid_cells = lat_rows * lon_cols
    live_slots = jnp.arange(slot_count, dtype=jnp.int32)[None, :] < sounding_count
    values = jnp.where(live_slots[:, None, :], sounding_forcing, 0.0)
    owner_ids = sounding_owner[:, :, 0]
    step_ids = jnp.arange(step_count, dtype=jnp.int32)[:, None]
    index_pair = jnp.stack([owner_ids, sounding_cell], axis=1)
    all_values, all_pairs = (
        lax.all_gather(values, ("lon", "lat"), axis=2, tiled=True),
        lax.all_gather(index_pair, ("lon", "lat"), axis=2, tiled=True),
    )
    kept_values = jnp.where((all_pairs[:, 0, :] == owner_self)[:, None, :], all_values, 0.0)
    target_cells = all_pairs[:, 1, :]
    forcing_grid = (
        jnp.zeros((step_count, lev_dev, grid_cells), jnp.float32)
        .at[step_ids, :, target_cells]
        .add(jnp.swapaxes(kept_values, 1, 2))
    )
    forcing_grid = forcing_grid.reshape(step_count, lev_dev, lat_rows, lon_cols)
    west_column = from_behind(east_courant[:, :, -1:], "lon", 1)
    west_wind = jnp.concatenate([west_column, east_courant[:, :, :-1]], axis=2)
    south_row = from_behind_2(north_courant[:, -1:, :], "lat", 1)
    south_wind = jnp.concatenate([south_row, north_courant[:, :-1, :]], axis=1)
    pole_pair = jnp.stack([north_courant[:, -1, :], pole_courant], axis=0)
    partner_winds = from_behind(pole_pair, "lon", lon_count // 2)
    row_index = jnp.arange(lat_rows, dtype=jnp.int32)[None, :, None]
    at_top = jnp.logical_and(lat_place == lat_count - 1, row_index == lat_rows - 1)
    at_bottom = jnp.logical_and(lat_place == 0, row_index == 0)
    upwind_east = jnp.maximum(east_courant, 0.0)
    upwind_west = -jnp.minimum(west_wind, 0.0)
    upwind_north = jnp.maximum(north_courant, 0.0) + jnp.where(
        at_top, -jnp.minimum(partner_winds[0], 0.0)[:, None, :], 0.0
    )
    upwind_south = jnp.where(
        at_bottom,
        (jnp.maximum(pole_courant, 0.0) - jnp.minimum(partner_winds[1], 0.0))[:, None, :],
        -jnp.minimum(south_wind, 0.0),
    )
    total_detrain = lax.psum(jnp.sum(detrain_share, axis=0), "lev")
    adjoint = adjoint_field
    for position in range(step_count):
        step_now = step_count - 1 - position
        adjoint = adjoint + forcing_grid[step_now][None]
        partial_sum = jnp.sum(detrain_share[None] * adjoint, axis=1)
        column_sum = mix_sum(partial_sum)
        adjoint = (1.0 - mix_fraction)[None] * adjoint + mix_fraction[None] * (
            column_sum / total_detrain
        )[:, None]
        across = extended(adjoint, (("lon", 3),), 1, True)
        east_side = across[:, :, :, 2:]
        west_side = across[:, :, :, :-2]
        upright = extended(adjoint, (("lat", 2),), 1, False)
        north_side = upright[:, :, 2:, :]
        south_side = upright[:, :, :-2, :]
        edge_row = jnp.where(lat_place == 0, adjoint[:, :, :1, :], adjoint[:, :, -1:, :])
        partner_row = from_behind(edge_row, "lon", lon_count // 2)
        north_side = jnp.where(at_top, partner_row, north_side)
        south_side = jnp.where(at_bottom, partner_row, south_side)
        adjoint = (
            adjoint
            + upwind_east * (east_side - adjoint)
            + upwind_west * (west_side - adjoint)
            + upwind_north * (north_side - adjoint)
            + upwind_south * (south_side - adjoint)
        )
    return adjoint


def solution(mesh):
    return jax.shard_map(
        on_device,
        mesh=mesh,
        in_specs=(
            P(None, "lev", "lat", "lon"),
            P("lev", "lat", "lon"),
            P("lev", "lat", "lon"),
            P("lev", "lon"),
            P("lev", "lat", "lon"),
            P("lev", "lat", "lon"),
            P(None, ("lon", "lat"), None),
            P(None, ("lon", "lat")),
            P(None, ("lon", "lat")),
            P(None, "lev", ("lon", "lat")),
        ),
        out_specs=P(None, "lev", "lat", "lon"),
        check_vma=False,
    )
```

profile of v0, /device:TPU:1, one launch (start us, length us, event | category | flops | bytes accessed | tf_op | source)
XLA Modules:
  0.0 865.7 jit_solution(10978872272690706526)
XLA Ops:
  6.5 0.7 copy.54
  7.2 0.7 pad_add_fusion.1
  7.9 160.9 %all_gather.6 = s32[2,2,32768]{2,0,1:T(2,128)S(1)} all-gather(s32[2,2,256]{2,0,1:T(2,128)S(1)} %pad_add_fusion.1), channel_id=1, replica_groups=mesh['lon'=32,'lat'=4,'lev'=4] {'lon','lat'}, dimensions={2}, use_global_device_ids=true | all-gather | bytes 528384 | tf_op jit(solution)/shard_map/all_gather | solution.py:63
  169.1 1.1 multiply_reduce_fusion.1
  170.3 1.4 and_reduce_fusion
  172.1 153.2 %all_gather.7 = f32[2,3,32768]{2,0,1:T(2,128)S(1)} all-gather(f32[2,3,256]{2,0,1:T(2,128)S(1)} %broadcast_select_fusion.2), channel_id=1, replica_groups=mesh['lon'=32,'lat'=4,'lev'=4] {'lon','lat'}, dimensions={2}, use_global_device_ids=true | all-gather | bytes 792576 | tf_op jit(solution)/shard_map/all_gather | solution.py:62
  325.3 0.5 select_bitcast_fusion
  325.8 16.6 %copy.38 = f32[2,32768,3]{2,1,0:T(8,128)} copy(f32[2,32768,3]{1,0,2:T(2,128)S(1)} %select_bitcast_fusion) | data formatting | bytes 1572864 | tf_op jit(solution)/shard_map/transpose | solution.py:70
  342.3 349.8 %scatter_custom_fusion = f32[3,8192]{0,1:T(8,128)} fusion(s32[65536]{0:T(1024)S(1)} %bitcast.41, f32[65536,3]{1,0:T(8,128)} %bitcast.36, f32[]{:T(128)} %constant.12.clone.1), kind=kCustom, calls=%fused_computation.1 | custom fusion | flops 196608 | bytes 98816
  692.1 3.9 fusion.43
  696.0 2.2 copy.24
  698.3 1.1 fusion.34
  699.5 3.4 collective-permute-start.6
  702.9 1.9 collective-permute-start.3
  704.9 1.9 collective-permute-start.1
  706.9 21.0 %psum.22 = f32[32,128]{1,0:T(8,128)S(1)} all-reduce(f32[32,128]{1,0:T(8,128)S(1)} %reduce_sum.28), channel_id=1, replica_groups=mesh['lon'=32,'lat'=4,'lev'=4] {'lev'}, use_global_device_ids=true, to_apply=%region_4.5 | all-reduce | flops 4096 | bytes 32768 | tf_op jit(solution)/shard_map/psum | solution.py:92
  727.9 0.6 copy.32
  728.7 21.9 %all-reduce.3.cloned.1.call-done = f32[12,32,128]{2,0,1:T(8,128)} async-done(((f32[12,32,128]{2,0,1:T(8,128)}), f32[12,32,128]{2,0,1:T(8,128)}) %all-reduce.3.cloned.1.call-update) | async-done | bytes 196624 | tf_op jit(solution)/shard_map/psum | solution.py:33
  750.6 1.0 broadcast_divide_fusion.1
  751.6 0.5 fusion.33
  752.1 0.3 fusion.45
  752.4 4.6 collective-permute-start.4
  757.0 4.9 collective-permute-start.5
  761.9 2.3 collective-permute-start.7
  764.2 0.3 copy.26
  764.5 5.2 collective-permute-start
  769.8 0.3 copy.28
  770.1 1.9 collective-permute-start.2
  772.1 0.4 copy.27
  772.5 5.4 collective-permute-done.2
  777.9 0.4 copy.29
  778.4 0.6 copy-done.5
  779.0 0.6 copy-done.7
  779.6 2.3 multiply_reduce_fusion
  781.9 47.8 %all-reduce.5.cloned.1.call-done = f32[12,32,128]{2,0,1:T(8,128)} async-done(((f32[12,32,128]{2,0,1:T(8,128)}), f32[12,32,128]{2,0,1:T(8,128)}) %all-reduce.5.cloned.1.call-update) | async-done | bytes 196624 | tf_op jit(solution)/shard_map/psum | solution.py:33
  829.8 1.0 broadcast_divide_fusion
  830.9 4.6 collective-permute-start.10
  835.5 4.9 collective-permute-start.11
  840.5 2.3 collective-permute-start.12
  843.0 0.3 copy.33
  843.4 5.1 collective-permute-start.8
  848.4 0.3 copy.35
  848.8 1.9 collective-permute-start.9
  850.7 0.4 copy.34
  851.1 5.5 collective-permute-done.9
  856.6 0.4 copy.36
  857.0 0.8 fusion.5
  857.8 1.0 copy.37
  (68 shorter events, 1.6 us)
Async XLA Ops:
  6.5 165.5 %copy-start.14 = (s32[2,1]{0,1:T(1,128)S(1)}, s32[2,1]{0,1:T(1,128)}, u32[]{:S(2)}) copy-start(s32[2,1]{0,1:T(1,128)} %param.18) | copy-start | bytes 28
  6.5 165.6 %copy-start.13 = (f32[2,3,256]{2,0,1:T(2,128)S(1)}, f32[2,3,256]{2,0,1:T(2,128)}, u32[]{:S(2)}) copy-start(f32[2,3,256]{2,0,1:T(2,128)} %param.19) | copy-start | bytes 18436
  6.5 744.1 %all-reduce.3.cloned.1.call-start = ((), (), s32[]{:S(2)}) async-start(), calls=%async_computation | async-start | bytes 524288 | tf_op jit(solution)/shard_map/psum | solution.py:33
  692.1 6.1 copy-start
  692.1 6.1 copy-start.1
  692.1 7.3 copy-start.4
  692.1 10.7 %copy-start.12 = (f32[3,128]{1,0:T(4,128)S(1)}, f32[3,128]{1,0:T(4,128)}, u32[]{:S(2)}) copy-start(f32[3,128]{1,0:T(4,128)} %param.13) | copy-start | bytes 4612
  692.1 12.7 %copy-start.2 = (f32[3,32,128]{2,1,0:T(8,128)S(1)}, f32[3,32,128]{2,1,0:T(8,128)}, u32[]{:S(2)}) copy-start(f32[3,32,128]{2,1,0:T(8,128)} %param.11) | copy-start | bytes 147460
  692.1 14.7 %copy-start.3 = (f32[3,32,128]{2,1,0:T(8,128)S(1)}, f32[3,32,128]{2,1,0:T(8,128)}, u32[]{:S(2)}) copy-start(f32[3,32,128]{2,1,0:T(8,128)} %param.14) | copy-start | bytes 147460
  699.4 130.4 %all-reduce.5.cloned.1.call-start = ((), (), s32[]{:S(2)}) async-start(), calls=%async_computation.1 | async-start | bytes 524288 | tf_op jit(solution)/shard_map/psum | solution.py:33
  699.5 29.1 %collective-permute-start.6 = (f32[3,1,128]{2,0,1:T(4,128)S(1)}, f32[3,1,128]{2,0,1:T(4,128)S(1)}, u32[]{:S(2)}, u32[]{:S(2)}) collective-permute-start(f32[3,1,128]{2,0,1:T(4,128)S(1)} %copy.55), channel_id=1, source_target_pairs={{0,4},{4,8},{8,12},{1,5},{5,9},{9,13},{2,6},{6,10},{10,14},{3,7},{... | collective-permute-start | bytes 4616 | tf_op jit(solution)/shard_map/ppermute | solution.py:16
  702.9 25.8 %collective-permute-start.3 = (f32[2,3,128]{2,1,0:T(4,128)S(1)}, f32[2,3,128]{2,1,0:T(4,128)S(1)}, u32[]{:S(2)}, u32[]{:S(2)}) collective-permute-start(f32[2,3,128]{2,1,0:T(4,128)S(1)} %pad_maximum_fusion.8), channel_id=1, source_target_pairs={{0,256},{16,272},{32,288},{48,304},{64,320},{80,336},{96,352},{112... | collective-permute-start | bytes 9224 | tf_op jit(solution)/shard_map/ppermute | solution.py:10
  704.9 23.6 %collective-permute-start.1 = (f32[3,32,1]{2,1,0:T(8,128)S(1)}, f32[3,32,1]{2,1,0:T(8,128)S(1)}, u32[]{:S(2)}, u32[]{:S(2)}) collective-permute-start(f32[3,32,1]{2,1,0:T(8,128)S(1)} %slice.98), channel_id=1, source_target_pairs={{0,16},{16,32},{32,48},{48,64},{64,80},{80,96},{96,112},{112,128},... | collective-permute-start | bytes 1160 | tf_op jit(solution)/shard_map/ppermute | solution.py:10
  706.9 57.7 %copy-start.10 = (pred[32]{0:T(512)(128)(4,1)}, pred[32]{0:T(512)(128)(4,1)S(1)}, u32[]{:S(2)}) copy-start(pred[32]{0:T(512)(128)(4,1)S(1)} %get-tuple-element.22) | copy-start | bytes 100
  706.9 65.1 %copy-start.8 = (pred[32]{0:T(512)(128)(4,1)}, pred[32]{0:T(512)(128)(4,1)S(1)}, u32[]{:S(2)}) copy-start(pred[32]{0:T(512)(128)(4,1)S(1)} %get-tuple-element.21) | copy-start | bytes 100
  752.4 26.0 %collective-permute-start.4 = (f32[12,3,1,128]{3,0,2,1:T(8,128)S(1)}, f32[12,3,1,128]{3,0,2,1:T(8,128)S(1)}, u32[]{:S(2)}, u32[]{:S(2)}) collective-permute-start(f32[12,3,1,128]{3,0,2,1:T(8,128)S(1)} %get-tuple-element.16), channel_id=1, source_target_pairs={{0,256},{16,272},{32,288},{48,304},{64,320},{80,336},{96,352},{112... | collective-permute-start | bytes 55304 | tf_op jit(solution)/shard_map/ppermute | solution.py:10
  757.0 21.4 %collective-permute-start.5 = (f32[12,3,1,128]{3,0,2,1:T(8,128)S(1)}, f32[12,3,1,128]{3,0,2,1:T(8,128)S(1)}, u32[]{:S(2)}, u32[]{:S(2)}) collective-permute-start(f32[12,3,1,128]{3,0,2,1:T(8,128)S(1)} %get-tuple-element.18), channel_id=1, source_target_pairs={{4,0},{8,4},{12,8},{5,1},{9,5},{13,9},{6,2},{10,6},{14,10},{7,3},{... | collective-permute-start | bytes 55304 | tf_op jit(solution)/shard_map/ppermute | solution.py:27
  761.9 16.5 %collective-permute-start.7 = (f32[12,3,1,128]{3,0,2,1:T(8,128)S(1)}, f32[12,3,1,128]{3,0,2,1:T(8,128)S(1)}, u32[]{:S(2)}, u32[]{:S(2)}) collective-permute-start(f32[12,3,1,128]{3,0,2,1:T(8,128)S(1)} %get-tuple-element.17), channel_id=1, source_target_pairs={{0,4},{4,8},{8,12},{1,5},{5,9},{9,13},{2,6},{6,10},{10,14},{3,7},{... | collective-permute-start | bytes 55304 | tf_op jit(solution)/shard_map/ppermute | solution.py:26
  764.5 7.6 collective-permute-start
  770.1 7.8 collective-permute-start.2
  778.4 0.6 copy-start.5
  778.4 0.6 copy-start.6
  779.0 0.6 copy-start.7
  830.8 26.3 %copy-start.9 = (pred[32]{0:T(512)(128)(4,1)S(1)}, pred[32]{0:T(512)(128)(4,1)}, u32[]{:S(2)}) copy-start(pred[32]{0:T(512)(128)(4,1)} %copy-done.8) | copy-start | bytes 100
  830.8 26.3 %copy-start.11 = (pred[32]{0:T(512)(128)(4,1)S(1)}, pred[32]{0:T(512)(128)(4,1)}, u32[]{:S(2)}) copy-start(pred[32]{0:T(512)(128)(4,1)} %copy-done.10) | copy-start | bytes 100
  830.9 26.1 %collective-permute-start.10 = (f32[12,3,1,128]{3,0,2,1:T(8,128)S(1)}, f32[12,3,1,128]{3,0,2,1:T(8,128)S(1)}, u32[]{:S(2)}, u32[]{:S(2)}) collective-permute-start(f32[12,3,1,128]{3,0,2,1:T(8,128)S(1)} %get-tuple-element.9), channel_id=1, source_target_pairs={{0,256},{16,272},{32,288},{48,304},{64,320},{80,336},{96,352},{112... | collective-permute-start | bytes 55304 | tf_op jit(solution)/shard_map/ppermute | solution.py:10
  835.5 21.5 %collective-permute-start.11 = (f32[12,3,1,128]{3,0,2,1:T(8,128)S(1)}, f32[12,3,1,128]{3,0,2,1:T(8,128)S(1)}, u32[]{:S(2)}, u32[]{:S(2)}) collective-permute-start(f32[12,3,1,128]{3,0,2,1:T(8,128)S(1)} %get-tuple-element.11), channel_id=1, source_target_pairs={{4,0},{8,4},{12,8},{5,1},{9,5},{13,9},{6,2},{10,6},{14,10},{7,3},{... | collective-permute-start | bytes 55304 | tf_op jit(solution)/shard_map/ppermute | solution.py:27
  840.5 16.6 %collective-permute-start.12 = (f32[12,3,1,128]{3,0,2,1:T(8,128)S(1)}, f32[12,3,1,128]{3,0,2,1:T(8,128)S(1)}, u32[]{:S(2)}, u32[]{:S(2)}) collective-permute-start(f32[12,3,1,128]{3,0,2,1:T(8,128)S(1)} %get-tuple-element.10), channel_id=1, source_target_pairs={{0,4},{4,8},{8,12},{1,5},{5,9},{9,13},{2,6},{6,10},{10,14},{3,7},{... | collective-permute-start | bytes 55304 | tf_op jit(solution)/shard_map/ppermute | solution.py:26
  843.4 7.3 collective-permute-start.8
  848.8 7.8 collective-permute-start.9
Sparse Core Ops, SparseCore 0:
  699.5 51.0 all-reduce.2
  782.1 47.6 all-reduce.4
where the time goes:
time: 866 us
  other arithmetic  361 us (42%)
  blocking collectives  335 us (39%)
  waiting for transfers between devices  80.7 us (9%)
  starting transfers between devices  44.9 us (5%)
  local copies, waits for them, and re-layouts  30 us (3%)
  between operations  13.9 us (2%)
    unnamed x4, other arithmetic  352 us
    all_gather x1, blocking collectives, on_device(): lax.all_gather(index_pair, ('lon', 'lat'), axis=2, tiled=True)  161 us
    all_gather x1, blocking collectives, on_device(): lax.all_gather(values, ('lon', 'lat'), axis=2, tiled=True)  153 us
    psum x2, waiting for transfers between devices, mix_sum(): return lax.psum(partial_sum, 'lev')  69.7 us
    psum x1, blocking collectives, on_device(): total_detrain = lax.psum(jnp.sum(detrain_share, axis=0), 'lev')  21 us
    ppermute x4, starting transfers between devices, extended(): after = lax.ppermute(initial, axis, down)  20.2 us
  transfers between devices with their start and end apart: 15, of which 4 were waited for; matrix products, arithmetic and copies ran while one was open for 0% of the time, Pallas kernels for 0%

commit v1 on v0

--- a/solution.py
+++ b/solution.py
@@ -60,7 +60,12 @@
     index_pair = jnp.stack([owner_ids, sounding_cell], axis=1)
     all_values, all_pairs = (
         lax.all_gather(values, ("lon", "lat"), axis=2, tiled=True),
-        lax.all_gather(index_pair, ("lon", "lat"), axis=2, tiled=True),
+        jnp.concatenate(
+            lax.all_to_all(
+                jnp.stack([index_pair] * lax.axis_size(("lon", "lat"))), ("lon", "lat"), 0, 0
+            ),
+            axis=2,
+        ),
     )
     kept_values = jnp.where((all_pairs[:, 0, :] == owner_self)[:, None, :], all_values, 0.0)
     target_cells = all_pairs[:, 1, :]

time: 866 us -> 770 us (0.89)
  blocking collectives: 335 us -> 181 us
  waiting for transfers between devices: 80.7 us -> 103 us
  starting transfers between devices: 44.9 us -> 63.3 us
  other arithmetic: 361 us -> 372 us
    all_gather x1 -> x0, blocking collectives: 161 us -> none  [on_device(): lax.all_gather(index_pair, ('lon', 'lat'), axis=2, tiled=True)]
    psum x2, waiting for transfers between devices: 69.7 us -> 93.1 us  [mix_sum(): return lax.psum(partial_sum, 'lev')]
    all_to_all x0 -> x1, starting transfers between devices: none -> 14.2 us  [on_device(): lax.all_to_all(jnp.stack([index_pair] * lax.axis_size(('lon', 'lat'))), (...]
  transfers between devices with their start and end apart: 15 -> 16, of which waited for: 4 -> 4; matrix products, arithmetic and copies ran while one was open for 0% -> 2% of each run, Pallas kernels for 0% -> 0%
where the time goes in v1:
time: 770 us; the launch traced here: 768 us
  other arithmetic  372 us (48%)
  blocking collectives  181 us (24%)
  waiting for transfers between devices  103 us (13%)
  starting transfers between devices  63.3 us (8%)
  local copies, waits for them, and re-layouts  35.3 us (5%)
  between operations  13.9 us (2%)
    unnamed x4, other arithmetic  352 us
    all_gather x1, blocking collectives, on_device(): lax.all_gather(values, ('lon', 'lat'), axis=2, tiled=True)  161 us
    psum x2, waiting for transfers between devices, mix_sum(): return lax.psum(partial_sum, 'lev')  93.1 us
    psum x1, blocking collectives, on_device(): total_detrain = lax.psum(jnp.sum(detrain_share, axis=0), 'lev')  20.3 us
    ppermute x4, starting transfers between devices, extended(): after = lax.ppermute(initial, axis, down)  20 us
    ppermute x4, starting transfers between devices, from_behind(): return lax.ppermute(value, axis, pairs)  17.1 us
    transpose x1, local copies, waits for them, and re-layouts, on_device(): jnp.swapaxes(kept_values, 1, 2)  16.5 us
  transfers between devices with their start and end apart: 16, of which 4 were waited for; matrix products, arithmetic and copies ran while one was open for 2% of the time, Pallas kernels for 0%

profile of v1, /device:TPU:1, one launch (start us, length us, event | category | flops | bytes accessed | tf_op | source)
XLA Modules:
  0.0 768.2 jit_solution(7541160854112384592)
XLA Ops:
  6.5 0.7 copy.89
  7.9 0.9 stack.12
  8.9 14.2 %all-to-all-start = ((s32[128,2,2,256]{3,1,2,0:T(2,128)}), s32[128,2,2,256]{3,1,2,0:T(2,128)S(1)}, u32[]{:S(2)}, u32[]{:S(2)}) async-start(s32[128,2,2,256]{3,1,2,0:T(2,128)} %stack.12), calls=%async_computation | async-start | bytes 1048576 | tf_op jit(solution)/shard_map/all_to_all | solution.py:64
  23.1 0.7 slice.102
  23.9 3.5 collective-permute-start.6
  28.1 4.9 collective-permute-start.3
  33.0 0.9 slice.98
  33.9 3.1 collective-permute-start.1
  37.0 0.8 broadcast_maximum_fusion
  37.8 0.7 iota_compare_fusion
  38.5 0.8 reduce_sum.28
  39.3 20.3 %psum.22 = f32[32,128]{1,0:T(8,128)S(1)} all-reduce(f32[32,128]{1,0:T(8,128)S(1)} %reduce_sum.28), channel_id=1, replica_groups=mesh['lon'=32,'lat'=4,'lev'=4] {'lev'}, use_global_device_ids=true, to_apply=%region_4.5 | all-reduce | flops 4096 | bytes 32768 | tf_op jit(solution)/shard_map/psum | solution.py:97
  59.6 1.4 broadcast_subtract_fusion
  61.8 160.9 %all_gather.3 = f32[2,3,32768]{2,0,1:T(2,128)S(1)} all-gather(f32[2,3,256]{2,0,1:T(2,128)S(1)} %broadcast_select_fusion.2), channel_id=1, replica_groups=mesh['lon'=32,'lat'=4,'lev'=4] {'lon','lat'}, dimensions={2}, use_global_device_ids=true | all-gather | bytes 792576 | tf_op jit(solution)/shard_map/all_gather | solution.py:62
  222.7 1.5 fusion.35
  224.2 1.5 select_add_fusion
  226.7 1.1 multiply_reduce_fusion.1
  227.8 1.3 and_reduce_fusion
  230.3 16.5 %copy.70 = f32[2,32768,3]{2,1,0:T(8,128)} copy(f32[2,32768,3]{1,0,2:T(2,128)S(1)} %select_bitcast_fusion) | data formatting | bytes 1572864 | tf_op jit(solution)/shard_map/transpose | solution.py:75
  246.8 349.8 %scatter_custom_fusion = f32[3,8192]{0,1:T(8,128)} fusion(s32[65536]{0:T(1024)S(1)} %bitcast.47, f32[65536,3]{1,0:T(8,128)} %bitcast.40, f32[]{:T(128)} %constant.12.clone.1), kind=kCustom, calls=%fused_computation.1 | custom fusion | flops 196608 | bytes 98816
  596.5 3.9 fusion.43
  600.4 2.2 copy.56
  602.7 1.1 fusion.34
  603.9 45.2 %all-reduce.3.cloned.1.call-done = f32[12,32,128]{2,0,1:T(8,128)} async-done(((f32[12,32,128]{2,0,1:T(8,128)}), f32[12,32,128]{2,0,1:T(8,128)}) %all-reduce.3.cloned.1.call-update) | async-done | bytes 196624 | tf_op jit(solution)/shard_map/psum | solution.py:33
  649.1 1.0 broadcast_divide_fusion.1
  650.1 1.3 fusion.33
  651.4 1.4 fusion.45
  652.9 4.6 collective-permute-start.4
  657.4 4.9 collective-permute-start.5
  662.4 2.3 collective-permute-start.7
  664.7 1.4 copy.58
  666.1 5.0 collective-permute-start
  671.2 1.4 copy.60
  672.6 1.9 collective-permute-start.2
  674.5 0.9 fusion.37
  676.5 4.0 collective-permute-done.2
  680.9 2.4 multiply_reduce_fusion
  683.4 47.8 %all-reduce.5.cloned.1.call-done = f32[12,32,128]{2,0,1:T(8,128)} async-done(((f32[12,32,128]{2,0,1:T(8,128)}), f32[12,32,128]{2,0,1:T(8,128)}) %all-reduce.5.cloned.1.call-update) | async-done | bytes 196624 | tf_op jit(solution)/shard_map/psum | solution.py:33
  731.2 1.0 broadcast_divide_fusion
  732.2 1.3 multiply_add_fusion
  733.5 4.6 collective-permute-start.10
  738.1 4.9 collective-permute-start.11
  743.0 2.3 collective-permute-start.12
  745.9 5.1 collective-permute-start.8
  751.3 1.9 collective-permute-start.9
  753.7 5.5 collective-permute-done.9
  759.6 0.8 fusion.5
  760.4 1.0 copy.69
  (65 shorter events, 7.7 us)
Async XLA Ops:
  6.5 220.1 %copy-start.10 = (s32[2]{0:T(128)S(1)}, s32[2]{0:T(128)}, u32[]{:S(2)}) copy-start(s32[2]{0:T(128)} %constant.41) | copy-start | bytes 28
  6.5 221.2 %copy-start.9 = (s32[2]{0:T(128)S(1)}, s32[2]{0:T(128)}, u32[]{:S(2)}) copy-start(s32[2]{0:T(128)} %constant.44) | copy-start | bytes 28
  8.9 216.8 %all-to-all-start = ((s32[128,2,2,256]{3,1,2,0:T(2,128)}), s32[128,2,2,256]{3,1,2,0:T(2,128)S(1)}, u32[]{:S(2)}, u32[]{:S(2)}) async-start(s32[128,2,2,256]{3,1,2,0:T(2,128)} %stack.12), calls=%async_computation | async-start | bytes 1048576 | tf_op jit(solution)/shard_map/all_to_all | solution.py:64
  23.1 626.0 %all-reduce.3.cloned.1.call-start = ((), (), s32[]{:S(2)}) async-start(), calls=%async_computation.1 | async-start | bytes 524288 | tf_op jit(solution)/shard_map/psum | solution.py:33
  23.9 200.3 %collective-permute-start.6 = (f32[3,1,128]{2,0,1:T(4,128)S(1)}, f32[3,1,128]{2,0,1:T(4,128)S(1)}, u32[]{:S(2)}, u32[]{:S(2)}) collective-permute-start(f32[3,1,128]{2,0,1:T(4,128)S(1)} %copy.90), channel_id=1, source_target_pairs={{0,4},{4,8},{8,12},{1,5},{5,9},{9,13},{2,6},{6,10},{10,14},{3,7},{... | collective-permute-start | bytes 4616 | tf_op jit(solution)/shard_map/ppermute | solution.py:16
  28.1 196.1 %collective-permute-start.3 = (f32[2,3,128]{2,1,0:T(4,128)S(1)}, f32[2,3,128]{2,1,0:T(4,128)S(1)}, u32[]{:S(2)}, u32[]{:S(2)}) collective-permute-start(f32[2,3,128]{2,1,0:T(4,128)S(1)} %pad_maximum_fusion.8), channel_id=1, source_target_pairs={{0,256},{16,272},{32,288},{48,304},{64,320},{80,336},{96,352},{112... | collective-permute-start | bytes 9224 | tf_op jit(solution)/shard_map/ppermute | solution.py:10
  33.9 188.8 %collective-permute-start.1 = (f32[3,32,1]{2,1,0:T(8,128)S(1)}, f32[3,32,1]{2,1,0:T(8,128)S(1)}, u32[]{:S(2)}, u32[]{:S(2)}) collective-permute-start(f32[3,32,1]{2,1,0:T(8,128)S(1)} %slice.98), channel_id=1, source_target_pairs={{0,16},{16,32},{32,48},{48,64},{64,80},{80,96},{96,112},{112,128},... | collective-permute-start | bytes 1160 | tf_op jit(solution)/shard_map/ppermute | solution.py:10
  596.5 6.1 copy-start
  596.5 6.1 copy-start.2
  596.5 7.3 copy-start.8
  602.7 46.4 %copy-start.5 = (f32[3,32,128]{2,1,0:T(8,128)}, f32[3,32,128]{2,1,0:T(8,128)S(1)}, u32[]{:S(2)}) copy-start(f32[3,32,128]{2,1,0:T(8,128)S(1)} %copy.56) | copy-start | bytes 147460
  603.8 127.4 %all-reduce.5.cloned.1.call-start = ((), (), s32[]{:S(2)}) async-start(), calls=%async_computation.2 | async-start | bytes 524288 | tf_op jit(solution)/shard_map/psum | solution.py:33
  651.4 29.5 %copy-start.1 = (f32[3,32,128]{2,1,0:T(8,128)S(1)}, f32[3,32,128]{2,1,0:T(8,128)}, u32[]{:S(2)}) copy-start(f32[3,32,128]{2,1,0:T(8,128)} %select_add_fusion) | copy-start | bytes 147460
  651.4 29.5 %copy-start.3 = (f32[3,32,128]{2,1,0:T(8,128)S(1)}, f32[3,32,128]{2,1,0:T(8,128)}, u32[]{:S(2)}) copy-start(f32[3,32,128]{2,1,0:T(8,128)} %param.15) | copy-start | bytes 147460
  651.4 29.5 %copy-start.4 = (f32[3,32,128]{2,1,0:T(8,128)S(1)}, f32[3,32,128]{2,1,0:T(8,128)}, u32[]{:S(2)}) copy-start(f32[3,32,128]{2,1,0:T(8,128)} %fusion.35) | copy-start | bytes 147460
  652.9 28.0 %collective-permute-start.4 = (f32[12,3,1,128]{3,0,2,1:T(8,128)S(1)}, f32[12,3,1,128]{3,0,2,1:T(8,128)S(1)}, u32[]{:S(2)}, u32[]{:S(2)}) collective-permute-start(f32[12,3,1,128]{3,0,2,1:T(8,128)S(1)} %get-tuple-element.16), channel_id=1, source_target_pairs={{0,256},{16,272},{32,288},{48,304},{64,320},{80,336},{96,352},{112... | collective-permute-start | bytes 55304 | tf_op jit(solution)/shard_map/ppermute | solution.py:10
  657.4 23.4 %collective-permute-start.5 = (f32[12,3,1,128]{3,0,2,1:T(8,128)S(1)}, f32[12,3,1,128]{3,0,2,1:T(8,128)S(1)}, u32[]{:S(2)}, u32[]{:S(2)}) collective-permute-start(f32[12,3,1,128]{3,0,2,1:T(8,128)S(1)} %get-tuple-element.18), channel_id=1, source_target_pairs={{4,0},{8,4},{12,8},{5,1},{9,5},{13,9},{6,2},{10,6},{14,10},{7,3},{... | collective-permute-start | bytes 55304 | tf_op jit(solution)/shard_map/ppermute | solution.py:27
  662.4 18.5 %collective-permute-start.7 = (f32[12,3,1,128]{3,0,2,1:T(8,128)S(1)}, f32[12,3,1,128]{3,0,2,1:T(8,128)S(1)}, u32[]{:S(2)}, u32[]{:S(2)}) collective-permute-start(f32[12,3,1,128]{3,0,2,1:T(8,128)S(1)} %get-tuple-element.17), channel_id=1, source_target_pairs={{0,4},{4,8},{8,12},{1,5},{5,9},{9,13},{2,6},{6,10},{10,14},{3,7},{... | collective-permute-start | bytes 55304 | tf_op jit(solution)/shard_map/ppermute | solution.py:26
  666.1 9.9 %collective-permute-start = (f32[12,3,32,1]{2,3,1,0:T(1,128)S(1)}, f32[12,3,32,1]{2,3,1,0:T(1,128)S(1)}, u32[]{:S(2)}, u32[]{:S(2)}) collective-permute-start(f32[12,3,32,1]{2,3,1,0:T(1,128)S(1)} %copy.58), channel_id=1, source_target_pairs={{16,0},{32,16},{48,32},{64,48},{80,64},{96,80},{112,96},{128,112},... | collective-permute-start | bytes 13832 | tf_op jit(solution)/shard_map/ppermute | solution.py:27
  672.6 7.8 %collective-permute-start.2 = (f32[12,3,32,1]{2,3,1,0:T(1,128)S(1)}, f32[12,3,32,1]{2,3,1,0:T(1,128)S(1)}, u32[]{:S(2)}, u32[]{:S(2)}) collective-permute-start(f32[12,3,32,1]{2,3,1,0:T(1,128)S(1)} %copy.60), channel_id=1, source_target_pairs={{0,16},{16,32},{32,48},{48,64},{64,80},{80,96},{96,112},{112,128},... | collective-permute-start | bytes 13832 | tf_op jit(solution)/shard_map/ppermute | solution.py:26
  675.4 56.8 %copy-start.6 = (f32[3,32,128]{2,1,0:T(8,128)S(1)}, f32[3,32,128]{2,1,0:T(8,128)}, u32[]{:S(2)}) copy-start(f32[3,32,128]{2,1,0:T(8,128)} %param.14) | copy-start | bytes 147460
  675.4 56.8 %copy-start.7 = (f32[3,32,128]{2,1,0:T(8,128)S(1)}, f32[3,32,128]{2,1,0:T(8,128)}, u32[]{:S(2)}) copy-start(f32[3,32,128]{2,1,0:T(8,128)} %broadcast_subtract_fusion) | copy-start | bytes 147460
  733.5 26.1 %collective-permute-start.10 = (f32[12,3,1,128]{3,0,2,1:T(8,128)S(1)}, f32[12,3,1,128]{3,0,2,1:T(8,128)S(1)}, u32[]{:S(2)}, u32[]{:S(2)}) collective-permute-start(f32[12,3,1,128]{3,0,2,1:T(8,128)S(1)} %get-tuple-element.9), channel_id=1, source_target_pairs={{0,256},{16,272},{32,288},{48,304},{64,320},{80,336},{96,352},{112... | collective-permute-start | bytes 55304 | tf_op jit(solution)/shard_map/ppermute | solution.py:10
  738.1 21.5 %collective-permute-start.11 = (f32[12,3,1,128]{3,0,2,1:T(8,128)S(1)}, f32[12,3,1,128]{3,0,2,1:T(8,128)S(1)}, u32[]{:S(2)}, u32[]{:S(2)}) collective-permute-start(f32[12,3,1,128]{3,0,2,1:T(8,128)S(1)} %get-tuple-element.11), channel_id=1, source_target_pairs={{4,0},{8,4},{12,8},{5,1},{9,5},{13,9},{6,2},{10,6},{14,10},{7,3},{... | collective-permute-start | bytes 55304 | tf_op jit(solution)/shard_map/ppermute | solution.py:27
  743.0 16.6 %collective-permute-start.12 = (f32[12,3,1,128]{3,0,2,1:T(8,128)S(1)}, f32[12,3,1,128]{3,0,2,1:T(8,128)S(1)}, u32[]{:S(2)}, u32[]{:S(2)}) collective-permute-start(f32[12,3,1,128]{3,0,2,1:T(8,128)S(1)} %get-tuple-element.10), channel_id=1, source_target_pairs={{0,4},{4,8},{8,12},{1,5},{5,9},{9,13},{2,6},{6,10},{10,14},{3,7},{... | collective-permute-start | bytes 55304 | tf_op jit(solution)/shard_map/ppermute | solution.py:26
  745.9 7.3 collective-permute-start.8
  751.3 7.8 %collective-permute-start.9 = (f32[12,3,32,1]{2,3,1,0:T(1,128)S(1)}, f32[12,3,32,1]{2,3,1,0:T(1,128)S(1)}, u32[]{:S(2)}, u32[]{:S(2)}) collective-permute-start(f32[12,3,32,1]{2,3,1,0:T(1,128)S(1)} %copy.67), channel_id=1, source_target_pairs={{0,16},{16,32},{32,48},{48,64},{64,80},{80,96},{96,112},{112,128},... | collective-permute-start | bytes 13832 | tf_op jit(solution)/shard_map/ppermute | solution.py:26
Sparse Core Ops, SparseCore 0:
  603.9 45.1 all-reduce.2
  683.5 47.6 all-reduce.4
